TPU v7x, 512 devices: a whole 4x8x8 slice. The times are simulated.
512 devices in a mesh: rep: 4 (over z_hi), fsdp: 128 (over z_lo, y, x, core).
Axes of the slice: x: 4, y: 8, z: 8 (z_hi: 4, z_lo: 2; z = z_hi * 2 + z_lo), core: 2. Of those that a mesh axis runs over, the one named last changes fastest.
Arguments:
- hidden: bfloat16 [4, 32768, 128], P('rep', 'fsdp'), may hold values from -4 to 4
- cotangent: bfloat16 [4, 32768, 8192], P('rep', 'fsdp'), may hold values from -0.0625 to 0.0625
- master: float32 [4, 128, 8192], P('rep', 'fsdp'), may hold values from -6 to 6
- adam_m: float32 [4, 128, 8192], P('rep', 'fsdp'), may hold values from -0.3125 to 0.3125
- adam_v: float32 [4, 128, 8192], P('rep', 'fsdp'), may hold values from 0.0005 to 0.008
- anchor: float32 [128, 8192], P('fsdp'), may hold values from -6 to 6
- outer_mom: float32 [128, 8192], P('fsdp'), may hold values from -1.75 to 1.75
- next_hidden: bfloat16 [4, 4096, 128], P('rep', 'fsdp'), may hold values from -0.5 to 0.5
Outputs:
- grad_hidden: bfloat16 [4, 32768, 128], P('rep', 'fsdp')
- merged: float32 [4, 128, 8192], P('rep', 'fsdp')
- new_anchor: float32 [128, 8192], P('fsdp')
- new_momentum: float32 [128, 8192], P('fsdp')
- next_out: bfloat16 [4, 4096, 8192], P('rep', 'fsdp')
All inputs are finite; a program needn't handle non-finite values.
Results may differ from a plain program's by a relative error of at most 0.018.
Values may be sent and summed in bfloat16 or wider, within the bound.
A program may use at most 64 MiB of HBM per device.

v0:
```python
import math
import jax
import jax.numpy as jnp
from jax import lax
from jax.sharding import PartitionSpec as P

BETA_ONE = 0.9
BETA_TWO = 0.95
INNER_LR = 0.3
DECAY = 0.1
EPS = 1e-08
OUTER_LR = 0.7
MOMENTUM = 0.9
ALPHA = 0.5
STEP = 100


def hadamard_table():
    index = jnp.arange(128, dtype=jnp.int32)
    count = jnp.zeros((128, 128), jnp.int32)
    for bit in range(7):
        left = jnp.bitwise_and(jnp.right_shift(index, bit), 1)
        count = count + left[:, None] * left[None, :]
    return (1 - 2 * (count % 2)).astype(jnp.float32)


def sign_vector(width):
    index = jnp.arange(width, dtype=jnp.int32)
    return (1 - 2 * (index * 97 % 251 % 2)).astype(jnp.float32)


def block_rotate(values, table):
    rows, width = values.shape
    blocks = values.reshape(rows, width // 128, 128)
    out = jnp.einsum("rbk,kj->rbj", blocks, table, precision=lax.Precision.HIGHEST)
    return out.reshape(rows, width) * (1.0 / math.sqrt(128.0))


def shards(hidden, cotangent, master, adam_m, adam_v, anchor, outer_mom, next_hidden):
    table = hadamard_table()
    width = master.shape[2]
    hidden_rows = hidden[0]
    cotangent_rows = cotangent[0]
    weights16 = master[0].astype(jnp.bfloat16)
    all_weights = lax.all_gather(weights16, "fsdp", axis=0, tiled=True)
    grad_hidden = lax.dot_general(
        cotangent_rows, all_weights, (((1,), (1,)), ((), ())), preferred_element_type=jnp.float32
    ).astype(jnp.bfloat16)
    full_grad = lax.dot_general(
        hidden_rows, cotangent_rows, (((0,), (0,)), ((), ())), preferred_element_type=jnp.float32
    )
    gradient = lax.psum_scatter(full_grad, "fsdp", scatter_dimension=0, tiled=True)
    corr_one = 1.0 - BETA_ONE**STEP
    corr_two = 1.0 - BETA_TWO**STEP
    first = BETA_ONE * adam_m[0] + (1.0 - BETA_ONE) * gradient
    second = BETA_TWO * adam_v[0] + (1.0 - BETA_TWO) * gradient * gradient
    update = first / corr_one / (jnp.sqrt(second / corr_two) + EPS) + DECAY * master[0]
    inner = master[0] - INNER_LR * update
    signs = sign_vector(width)
    rotated = block_rotate((anchor - inner) * signs[None, :], table).astype(jnp.bfloat16)
    replicas = lax.axis_size("rep")
    total = lax.psum(rotated.astype(jnp.float32).astype(jnp.bfloat16), "rep").astype(jnp.float32)
    mean_delta = block_rotate(total, table) * signs[None, :] / replicas
    new_momentum = MOMENTUM * outer_mom + mean_delta
    new_anchor = anchor - OUTER_LR * (MOMENTUM * new_momentum + mean_delta)
    merged = ALPHA * inner + (1.0 - ALPHA) * new_anchor
    merged16 = merged.astype(jnp.bfloat16)
    next_rows = next_hidden[0]
    all_merged = lax.all_gather(merged16, "fsdp", axis=0, tiled=True)
    next_out = jnp.dot(next_rows, all_merged, preferred_element_type=jnp.float32).astype(
        jnp.bfloat16
    )
    return (grad_hidden[None], merged[None], new_anchor, new_momentum, next_out[None])


def solution(mesh):
    in_specs = (
        P("rep", "fsdp", None),
        P("rep", "fsdp", None),
        P("rep", "fsdp", None),
        P("rep", "fsdp", None),
        P("rep", "fsdp", None),
        P("fsdp", None),
        P("fsdp", None),
        P("rep", "fsdp", None),
    )
    out_specs = (
        P("rep", "fsdp", None),
        P("rep", "fsdp", None),
        P("fsdp", None),
        P("fsdp", None),
        P("rep", "fsdp", None),
    )
    return jax.shard_map(shards, mesh=mesh, in_specs=in_specs, out_specs=out_specs, check_vma=False)
```

profile of v0, /device:TPU:8, one launch (start us, length us, event | category | flops | bytes accessed | tf_op | source)
XLA Modules:
  0.0 1570.5 jit_solution(18300237138548457707)
XLA Ops:
  7.2 0.0 copy-start
  7.2 0.0 all-reduce.3.cloned.1.call-start
  7.2 0.8 copy-done
  8.0 4.9 fusion.1
  12.9 0.0 all-reduce.3.cloned.1.call-update
  13.0 0.0 all-gather.5.cloned.1.call-start
  13.0 0.7 copy-done.3
  13.7 0.6 fusion.32
  14.3 0.0 all-gather.5.cloned.1.call-update
  14.3 0.0 all-gather.7.cloned.1.call-start
  14.4 1.3 dynamic-slice
  15.7 1087.4 %all-reduce.3.cloned.1.call-done = f32[128,8192]{1,0:T(8,128)} async-done(((f32[128,8192]{1,0:T(8,128)}), f32[128,8192]{1,0:T(8,128)}) %all-reduce.3.cloned.1.call-update) | async-done | bytes 4194320
  1103.1 2.1 subtract_multiply_fusion
  1105.2 0.0 copy-start.7
  1105.2 0.4 fusion.19
  1105.6 19.6 %psum.7 = bf16[64,128]{1,0:T(8,128)(2,1)S(1)} all-reduce(bf16[64,128]{1,0:T(8,128)(2,1)S(1)} %fusion.19), channel_id=1, replica_groups=mesh['rep'=4,'fsdp'=128] {'rep'}, use_global_device_ids=true, to_apply=%region_1.2 | all-reduce | flops 8192 | bytes 32768 | tf_op jit(solution)/shard_map/psum | solution.py:62
  1125.2 0.3 convolution_multiply_fusion
  1125.6 1.0 convert_bitcast_fusion
  1126.6 0.0 all-gather.7.cloned.1.call-update
  1126.6 211.1 %all-gather.5.cloned.1.call-done = bf16[128,1,8192]{2,1,0:T(2,128)(2,1)} async-done(((bf16[1,1,8192]{2,1,0:T(2,128)(2,1)}), bf16[128,1,8192]{2,1,0:T(2,128)(2,1)}) %all-gather.5.cloned.1.call-update) | async-done | bytes 2097168 | tf_op jit(solution)/shard_map/all_gather | solution.py:45
  1337.7 7.0 fusion.14
  1344.7 0.7 fusion.44
  1345.3 213.2 %all-gather.7.cloned.1.call-done = bf16[128,1,8192]{2,1,0:T(2,128)(2,1)} async-done(((bf16[1,1,8192]{2,1,0:T(2,128)(2,1)}), bf16[128,1,8192]{2,1,0:T(2,128)(2,1)}) %all-gather.7.cloned.1.call-update) | async-done | bytes 2097168 | tf_op jit(solution)/shard_map/all_gather | solution.py:69
  1558.6 5.4 fusion
  (16 shorter events, 0.0 us)
Async XLA Ops:
  7.2 0.8 copy-start
  7.2 1095.9 %all-reduce.3.cloned.1.call-start = ((), (), s32[]{:S(2)}) async-start(), calls=%async_computation.2 | async-start | bytes 8388608
  12.9 0.8 copy-start.3
  12.9 1090.2 %copy-start.1 = (f32[1,8192]{1,0:T(1,128)S(1)}, f32[1,8192]{1,0:T(1,128)}, u32[]{:S(2)}) copy-start(f32[1,8192]{1,0:T(1,128)} %param.13) | copy-start | bytes 98308
  12.9 1090.2 %copy-start.4 = (f32[1,1,8192]{2,1,0:T(1,128)S(1)}, f32[1,1,8192]{2,1,0:T(1,128)}, u32[]{:S(2)}) copy-start(f32[1,1,8192]{2,1,0:T(1,128)} %param.12) | copy-start | bytes 98308
  12.9 1090.2 %copy-start.5 = (f32[1,1,8192]{2,1,0:T(1,128)S(1)}, f32[1,1,8192]{2,1,0:T(1,128)}, u32[]{:S(2)}) copy-start(f32[1,1,8192]{2,1,0:T(1,128)} %param.11) | copy-start | bytes 98308
  12.9 1112.6 %copy-start.6 = (f32[1,8192]{1,0:T(1,128)S(1)}, f32[1,8192]{1,0:T(1,128)}, u32[]{:S(2)}) copy-start(f32[1,8192]{1,0:T(1,128)} %param.14) | copy-start | bytes 98308
  13.0 1324.7 %all-gather.5.cloned.1.call-start = ((), (), s32[]{:S(2)}) async-start(), calls=%async_computation | async-start | bytes 4227072 | tf_op jit(solution)/shard_map/all_gather | solution.py:45
  14.3 1544.2 %all-gather.7.cloned.1.call-start = ((), (), s32[]{:S(2)}) async-start(), calls=%async_computation.1 | async-start | bytes 4227072 | tf_op jit(solution)/shard_map/all_gather | solution.py:69
  1105.2 453.3 %copy-start.7 = (bf16[1,32,128]{2,1,0:T(8,128)(2,1)S(1)}, bf16[1,32,128]{2,1,0:T(8,128)(2,1)}, u32[]{:S(2)}) copy-start(bf16[1,32,128]{2,1,0:T(8,128)(2,1)} %param.15) | copy-start | bytes 24580
  1126.6 437.4 %copy-start.2 = (f32[1,8192]{1,0:T(1,128)}, f32[1,8192]{1,0:T(1,128)S(1)}, u32[]{:S(2)}) copy-start(f32[1,8192]{1,0:T(1,128)S(1)} %get-tuple-element.6) | copy-start | bytes 98308
Sparse Core Ops, SparseCore 0:
  13.1 1089.9 all-reduce.2
  1106.1 231.5 all-gather.4
  1340.7 217.8 all-gather.6
where the time goes:
time: 1570 us
  waiting for transfers between devices  1510 us (96%)
  blocking collectives  19.6 us (1%)
  matrix products  18 us (1%)
    unnamed x4, waiting for transfers between devices  1090 us
    all_gather x1, waiting for transfers between devices, shards(): all_merged = lax.all_gather(merged16, 'fsdp', axis=0, tiled=True)  213 us
    all_gather x1, waiting for transfers between devices, shards(): all_weights = lax.all_gather(weights16, 'fsdp', axis=0, tiled=True)  211 us
  transfers between devices with their start and end apart: 3, of which 3 were waited for; matrix products, arithmetic and copies ran while one was open for 1% of the time, Pallas kernels for 0%

commit v1 on v0

--- a/solution.py
+++ b/solution.py
@@ -66,7 +66,8 @@
     merged = ALPHA * inner + (1.0 - ALPHA) * new_anchor
     merged16 = merged.astype(jnp.bfloat16)
     next_rows = next_hidden[0]
-    all_merged = lax.all_gather(merged16, "fsdp", axis=0, tiled=True)
+    sent = jnp.stack([merged16] * lax.axis_size("fsdp"))
+    all_merged = jnp.concatenate(lax.all_to_all(sent, "fsdp", 0, 0), axis=0)
     next_out = jnp.dot(next_rows, all_merged, preferred_element_type=jnp.float32).astype(
         jnp.bfloat16
     )

time: 1570 us -> 1370 us (0.87)
  waiting for transfers between devices: 1510 us -> 1260 us
  starting transfers between devices: 0.12 us -> 25.2 us
  local copies, waits for them, and re-layouts: 2.75 us -> 18.9 us
    all_gather x1 -> x0, waiting for transfers between devices: 213 us -> none  [shards(): all_merged = lax.all_gather(merged16, 'fsdp', axis=0, tiled=True)]
    all_gather x1, waiting for transfers between devices: 211 us -> 172 us  [shards(): all_weights = lax.all_gather(weights16, 'fsdp', axis=0, tiled=True)]
    all_to_all x0 -> x1, starting transfers between devices: none -> 25.1 us  [shards(): all_merged = jnp.concatenate(lax.all_to_all(sent, 'fsdp', 0, 0), axis=0)]
    unnamed x4 -> x3, waiting for transfers between devices: 1090 us -> 1090 us
  transfers between devices with their start and end apart: 3 -> 3, of which waited for: 3 -> 2; matrix products, arithmetic and copies ran while one was open for 1% -> 3% of each run, Pallas kernels for 0% -> 0%
where the time goes in v1:
time: 1370 us
  waiting for transfers between devices  1260 us (92%)
  starting transfers between devices  25.2 us (2%)
  blocking collectives  19.6 us (1%)
  local copies, waits for them, and re-layouts  18.9 us (1%)
  matrix products  18 us (1%)
  other arithmetic  17.6 us (1%)
  between operations  14.2 us (1%)
    unnamed x3, waiting for transfers between devices  1090 us
    all_gather x1, waiting for transfers between devices, shards(): all_weights = lax.all_gather(weights16, 'fsdp', axis=0, tiled=True)  172 us
  transfers between devices with their start and end apart: 3, of which 2 were waited for; matrix products, arithmetic and copies ran while one was open for 3% of the time, Pallas kernels for 0%

profile of v1, /device:TPU:8, one launch (start us, length us, event | category | flops | bytes accessed | tf_op | source)
XLA Modules:
  0.0 1370.8 jit_solution(7404302678454090288)
XLA Ops:
  7.2 0.0 all-reduce.3.cloned.1.call-start
  7.2 0.8 copy-done
  8.0 4.9 fusion.1
  12.9 0.0 all-reduce.3.cloned.1.call-update
  13.0 0.0 all-gather.3.cloned.1.call-start
  13.0 0.7 copy-done.1
  13.7 0.6 fusion.32
  14.4 1.3 dynamic-slice
  15.7 1085.7 %all-reduce.3.cloned.1.call-done = f32[128,8192]{1,0:T(8,128)} async-done(((f32[128,8192]{1,0:T(8,128)}), f32[128,8192]{1,0:T(8,128)}) %all-reduce.3.cloned.1.call-update) | async-done | bytes 4194320
  1101.4 2.1 subtract_multiply_fusion
  1103.5 0.4 fusion.19
  1103.9 19.6 %psum.7 = bf16[64,128]{1,0:T(8,128)(2,1)S(1)} all-reduce(bf16[64,128]{1,0:T(8,128)(2,1)S(1)} %fusion.19), channel_id=1, replica_groups=mesh['rep'=4,'fsdp'=128] {'rep'}, use_global_device_ids=true, to_apply=%region_1.2 | all-reduce | flops 8192 | bytes 32768 | tf_op jit(solution)/shard_map/psum | solution.py:62
  1123.5 0.3 convolution_multiply_fusion
  1123.8 1.0 convert_reduce_fusion
  1124.8 6.2 stack.2
  1131.0 0.5 broadcast.364
  1131.5 13.2 reduce.2
  1144.7 2.8 reshape.271
  1147.5 25.1 %all-to-all-start = ((bf16[128,2,4096]{2,1,0:T(2,128)(2,1)}), bf16[128,2,4096]{2,1,0:T(2,128)(2,1)S(1)}, u32[]{:S(2)}, u32[]{:S(2)}) async-start(bf16[128,2,4096]{2,1,0:T(2,128)(2,1)} %reshape.271), calls=%async_computation | async-start | bytes 4194304 | tf_op jit(solution)/shard_map/all_to_all | solution.py:70
  1172.6 171.5 %all-gather.3.cloned.1.call-done = bf16[128,1,8192]{2,1,0:T(2,128)(2,1)} async-done(((bf16[1,1,8192]{2,1,0:T(2,128)(2,1)}), bf16[128,1,8192]{2,1,0:T(2,128)(2,1)}) %all-gather.3.cloned.1.call-update) | async-done | bytes 2097168 | tf_op jit(solution)/shard_map/all_gather | solution.py:45
  1344.2 7.0 fusion.14
  1351.1 0.7 fusion.44
  1351.8 6.7 reshape.272
  1358.5 5.4 fusion
  (20 shorter events, 0.1 us)
Async XLA Ops:
  7.2 0.8 copy-start
  7.2 1094.2 %all-reduce.3.cloned.1.call-start = ((), (), s32[]{:S(2)}) async-start(), calls=%async_computation.2 | async-start | bytes 8388608
  12.9 0.8 copy-start.1
  12.9 1088.5 %copy-start.2 = (f32[1,8192]{1,0:T(1,128)S(1)}, f32[1,8192]{1,0:T(1,128)}, u32[]{:S(2)}) copy-start(f32[1,8192]{1,0:T(1,128)} %param.13) | copy-start | bytes 98308
  12.9 1088.5 %copy-start.4 = (f32[1,1,8192]{2,1,0:T(1,128)S(1)}, f32[1,1,8192]{2,1,0:T(1,128)}, u32[]{:S(2)}) copy-start(f32[1,1,8192]{2,1,0:T(1,128)} %param.12) | copy-start | bytes 98308
  12.9 1088.5 %copy-start.5 = (f32[1,1,8192]{2,1,0:T(1,128)S(1)}, f32[1,1,8192]{2,1,0:T(1,128)}, u32[]{:S(2)}) copy-start(f32[1,1,8192]{2,1,0:T(1,128)} %param.11) | copy-start | bytes 98308
  12.9 1110.9 %copy-start.6 = (f32[1,8192]{1,0:T(1,128)S(1)}, f32[1,8192]{1,0:T(1,128)}, u32[]{:S(2)}) copy-start(f32[1,8192]{1,0:T(1,128)} %param.14) | copy-start | bytes 98308
  13.0 1331.2 %all-gather.3.cloned.1.call-start = ((), (), s32[]{:S(2)}) async-start(), calls=%async_computation.1 | async-start | bytes 4227072 | tf_op jit(solution)/shard_map/all_gather | solution.py:45
  1124.8 226.3 %copy-start.3 = (f32[1,8192]{1,0:T(1,128)}, f32[1,8192]{1,0:T(1,128)S(1)}, u32[]{:S(2)}) copy-start(f32[1,8192]{1,0:T(1,128)S(1)} %get-tuple-element.6) | copy-start | bytes 98308
  1147.5 204.3 %all-to-all-start = ((bf16[128,2,4096]{2,1,0:T(2,128)(2,1)}), bf16[128,2,4096]{2,1,0:T(2,128)(2,1)S(1)}, u32[]{:S(2)}, u32[]{:S(2)}) async-start(bf16[128,2,4096]{2,1,0:T(2,128)(2,1)} %reshape.271), calls=%async_computation | async-start | bytes 4194304 | tf_op jit(solution)/shard_map/all_to_all | solution.py:70
  1351.1 7.4 copy-start.7
Sparse Core Ops, SparseCore 0:
  13.1 1088.2 all-reduce.2
  1104.3 239.7 all-gather.2
